TPU v7x, 32 devices: a whole 2x2x4 slice. The times are simulated.
32 devices in a mesh: grp: 4 (over x, core), dev: 8 (over z, y).
Axes of the slice: x: 2, y: 2, z: 4, core: 2. Of those that a mesh axis runs over, the one named last changes fastest.
Arguments:
- features: bfloat16 [24576, 512], P(('grp', 'dev')), may hold values from -6 to 6
- grad_out: bfloat16 [24576, 512], P(('grp', 'dev')), may hold values from -6 to 6
- w_self: bfloat16 [512, 512], replicated, may hold values from -0.25 to 0.25
- w_neigh: bfloat16 [512, 512], replicated, may hold values from -0.25 to 0.25
- neighbours: int32 [24576, 32], P(('grp', 'dev')), may hold values from 0 to 895, as said below
- degree: int32 [24576], P(('grp', 'dev')), may hold values from 8 to 32
- send_rows: int32 [256, 8], P(('grp', 'dev')), may hold values from 0 to 767
- hub_rows: int32 [64], P(('grp', 'dev')), may hold values from 0 to 767, as said below
Outputs:
- output: bfloat16 [24576, 512], P(('grp', 'dev'))
- grad_features: bfloat16 [24576, 512], P(('grp', 'dev'))
Inputs may be any that keep to these rules, and one draw needn't show every extreme that they name: `neighbours`: codes below 768 name rows of the node's device, the next 64 name rows listed for it by its group, the last 64 name hub nodes. Slot 0 of every node holds a listed row and slot 1 a hub; every listed row of a device is named by some node of the reading device and every hub by some node. `hub_rows`: the 2 entries of one device are distinct rows of that device.
All inputs are finite; a program needn't handle non-finite values.
Results may differ from a plain program's by a relative error of at most 0.0051.
Values may be sent and summed in bfloat16 or wider, within the bound.
A program may use at most 64 MiB of HBM per device.

v0:
```python
import math

import jax
import jax.numpy as jnp
from jax import lax
from jax.sharding import PartitionSpec as P


def count_tiles(slot_codes, keep_mask, tile_width, first_code):
    column_ids = first_code + lax.iota(jnp.int32, tile_width)
    matches = (slot_codes[:, :, None] == column_ids[None, None, :]) & keep_mask[:, :, None]
    return jnp.sum(matches.astype(jnp.bfloat16), axis=1)


def local(features, grad_out, w_self, w_neigh, neighbours, degree, send_rows, hub_rows):
    row_count, feat_width = features.shape
    slot_count = neighbours.shape[1]
    groups = lax.axis_size("grp")
    members = lax.axis_size("dev")
    halo_count = send_rows.shape[0] * send_rows.shape[1]
    owned_hubs = hub_rows.shape[0]
    hub_count = owned_hubs * groups * members
    keep_slots = lax.iota(jnp.int32, slot_count)[None, :] < degree[:, None]
    block_rows = math.gcd(row_count, 256)
    block_total = row_count // block_rows

    def build_tiles(block_args):
        slot_codes, keep_mask = block_args
        return (
            count_tiles(slot_codes, keep_mask, row_count, 0),
            count_tiles(slot_codes, keep_mask, halo_count, row_count),
            count_tiles(slot_codes, keep_mask, hub_count, row_count + halo_count),
        )

    tile_local, tile_halo, tile_hub = lax.map(
        build_tiles,
        (
            neighbours.reshape(block_total, block_rows, slot_count),
            keep_slots.reshape(block_total, block_rows, slot_count),
        ),
    )
    tile_local = tile_local.reshape(row_count, row_count)
    tile_halo = tile_halo.reshape(row_count, halo_count)
    tile_hub = tile_hub.reshape(row_count, hub_count)
    send_list = send_rows.reshape(halo_count)
    outgoing = jnp.take(features, send_list, axis=0)
    incoming = lax.all_to_all(outgoing, "dev", split_axis=0, concat_axis=0, tiled=True)
    summed = jnp.dot(tile_local, features, preferred_element_type=jnp.float32)
    summed = summed + jnp.dot(tile_halo, incoming, preferred_element_type=jnp.float32)
    hub_own = jnp.take(features, hub_rows, axis=0)
    tile_cols = tile_hub
    summed = summed + jnp.dot(
        tile_cols,
        lax.all_gather(hub_own, ("grp", "dev"), axis=0, tiled=True),
        preferred_element_type=jnp.float32,
    )
    degree_f = degree.astype(jnp.float32)[:, None]
    neigh_mean = (summed / degree_f).astype(jnp.bfloat16)
    preact = jnp.dot(features, w_self, preferred_element_type=jnp.float32) + jnp.dot(
        neigh_mean, w_neigh, preferred_element_type=jnp.float32
    )
    output = jax.nn.silu(preact).astype(jnp.bfloat16)
    sigmoid_pre = jax.nn.sigmoid(preact)
    gated = (
        grad_out.astype(jnp.float32) * sigmoid_pre * (1.0 + preact * (1.0 - sigmoid_pre))
    ).astype(jnp.bfloat16)
    contract_last = (((1,), (1,)), ((), ()))
    contract_first = (((0,), (0,)), ((), ()))
    grad_self = lax.dot_general(gated, w_self, contract_last, preferred_element_type=jnp.float32)
    scaled = (
        lax.dot_general(gated, w_neigh, contract_last, preferred_element_type=jnp.float32)
        / degree_f
    ).astype(jnp.bfloat16)
    grad_total = grad_self + lax.dot_general(
        tile_local, scaled, contract_first, preferred_element_type=jnp.float32
    )
    halo_partial = lax.dot_general(
        tile_halo, scaled, contract_first, preferred_element_type=jnp.float32
    )
    returned = lax.all_to_all(
        halo_partial.astype(jnp.bfloat16), "dev", split_axis=0, concat_axis=0, tiled=True
    ).astype(halo_partial.dtype)
    grad_total = grad_total + jax.ops.segment_sum(returned, send_list, num_segments=row_count)
    tile_cols = tile_hub
    mine = lax.psum_scatter(
        lax.dot_general(tile_cols, scaled, contract_first, preferred_element_type=jnp.float32),
        ("grp", "dev"),
        scatter_dimension=0,
        tiled=True,
    )
    grad_total = grad_total + jax.ops.segment_sum(mine, hub_rows, num_segments=row_count)
    return (output, grad_total.astype(jnp.bfloat16))


def solution(mesh):
    placed = (
        P(("grp", "dev"), None),
        P(("grp", "dev"), None),
        P(),
        P(),
        P(("grp", "dev"), None),
        P(("grp", "dev")),
        P(("grp", "dev"), None),
        P(("grp", "dev")),
    )
    return jax.shard_map(
        local,
        mesh=mesh,
        in_specs=placed,
        out_specs=(P(("grp", "dev"), None), P(("grp", "dev"), None)),
        check_vma=False,
    )
```

profile of v0, /device:TPU:0, one launch (start us, length us, event | category | flops | bytes accessed | tf_op | source)
XLA Modules:
  0.0 273.5 jit_solution(13714239355453946839)
XLA Ops:
  7.2 0.8 reshape.95
  8.0 0.7 compare_and_fusion
  8.7 0.7 gather_fusion
  9.4 0.7 bitcast_select_fusion
  10.1 7.3 %all-to-all-start = ((bf16[8,8,512]{2,1,0:T(8,128)(2,1)}), bf16[8,8,512]{2,1,0:T(8,128)(2,1)S(1)}, u32[]{:S(2)}, u32[]{:S(2)}) async-start(bf16[8,8,512]{2,1,0:T(8,128)(2,1)} %bitcast_select_fusion), calls=%async_computation | async-start | bytes 131072 | tf_op jit(solution)/shard_map/all_to_all | solution.py:47
  17.5 0.7 compare_select_fusion.1
  18.1 0.7 compare_and_fusion.1
  18.8 0.9 reshape.92
  19.7 0.7 lt.49
  20.5 23.6 %while.17 = (s32[]{:T(128)}, bf16[3,256,768]{2,1,0:T(8,128)(2,1)S(1)}, bf16[3,256,64]{1,2,0:T(8,128)(2,1)S(1)}, bf16[3,256,64]{1,2,0:T(8,128)(2,1)S(1)}, s32[3,2...) while((s32[]{:T(128)}, bf16[3,256,768]{2,1,0:T(8,128)(2,1)S(1)}, ...), condition=%wide.region_4.5_spmd, body=%wide.region_0.4_spmd.sunk | while | flops 29130880 | bytes 1688669 | solution.py:35
  20.6 0.8 fusion.40
  21.6 6.7 %fusion.39 = bf16[256,768]{1,0:T(8,128)(2,1)S(1)} fusion(s32[256,32]{1,0:T(8,128)S(1)} %bitcast.64, pred[256,32]{1,0:T(8,128)(4,1)S(1)} %copy.29), kind=kLoop, calls=%fused_computation.6.clone.1 | loop fusion | flops 24969216 | bytes 434176 | tf_op jit(solution)/shard_map/while/body/eval_jaxpr/reduce_sum | solution.py:12
  28.4 0.8 fusion.40
  29.5 6.7 %fusion.39 = bf16[256,768]{1,0:T(8,128)(2,1)S(1)} fusion(s32[256,32]{1,0:T(8,128)S(1)} %bitcast.64, pred[256,32]{1,0:T(8,128)(4,1)S(1)} %copy.29), kind=kLoop, calls=%fused_computation.6.clone.1 | loop fusion | flops 24969216 | bytes 434176 | tf_op jit(solution)/shard_map/while/body/eval_jaxpr/reduce_sum | solution.py:12
  36.3 0.8 fusion.40
  37.3 6.7 %fusion.39 = bf16[256,768]{1,0:T(8,128)(2,1)S(1)} fusion(s32[256,32]{1,0:T(8,128)S(1)} %bitcast.64, pred[256,32]{1,0:T(8,128)(4,1)S(1)} %copy.29), kind=kLoop, calls=%fused_computation.6.clone.1 | loop fusion | flops 24969216 | bytes 434176 | tf_op jit(solution)/shard_map/while/body/eval_jaxpr/reduce_sum | solution.py:12
  44.1 1.0 copy-done.3
  45.1 1.9 fusion.16
  47.1 1.7 fusion.15
  49.5 68.1 %all-gather = bf16[32,2,512]{2,1,0:T(2,128)(2,1)S(1)} all-gather(bf16[1,2,512]{2,1,0:T(2,128)(2,1)S(1)} %fusion.13), channel_id=1, replica_groups=mesh['grp'=4,'dev'=8] {'grp','dev'}, dimensions={0}, use_global_device_ids=true | all-gather | bytes 67584 | tf_op jit(solution)/shard_map/all_gather | solution.py:54
  118.1 4.9 %multiply_convert_fusion = (bf16[768,512]{1,0:T(8,128)(2,1)}, bf16[768,512]{1,0:T(8,128)(2,1)}) fusion(bf16[768,512]{1,0:T(8,128)(2,1)} %param.11, f32[768,512]{1,0:T(8,128)} %fusion.15, bf16[512,512]{1,0:T(8,128)(2,1)} %param.13, f32[768,512]{1,0:T(8,128)} %fusion.16, f32[768,512]{1,0:T(8,128)S(1)} %fusion.11, bf16[768,64]{0,1:T(8,128)(2,1)S(1)} %bitcast.68, ...), kind=kOutput, calls=%fused_computation.20 | convolution fusion | flops 459669504 | bytes 7769088 | tf_op jit(solution)/shard_map/dot_general | solution.py:59
  123.0 2.0 divide_convert_fusion
  125.0 2.0 fusion.17
  127.0 0.9 fusion.5
  127.9 0.9 fusion.18
  128.8 3.3 %all-to-all-start.1 = ((bf16[8,8,512]{2,1,0:T(8,128)(2,1)}), bf16[8,8,512]{2,1,0:T(8,128)(2,1)S(1)}, u32[]{:S(2)}, u32[]{:S(2)}) async-start(bf16[8,8,512]{2,1,0:T(8,128)(2,1)} %fusion.5), calls=%async_computation.1 | async-start | bytes 131072 | tf_op jit(solution)/shard_map/all_to_all | solution.py:80
  132.2 0.7 all-reduce.3.cloned.1.call-update
  132.9 2.3 convolution_add_fusion
  135.1 128.2 %all-reduce.3.cloned.1.call-done = f32[64,512]{1,0:T(8,128)} async-done(((f32[64,512]{1,0:T(8,128)}), f32[64,512]{1,0:T(8,128)}) %all-reduce.3.cloned.1.call-update) | async-done | bytes 131088
  263.4 0.7 constant_dynamic-slice_fusion.1
  264.1 1.6 scatter_custom_fusion
  265.7 1.0 convert_element_type.66
  (57 shorter events, 2.2 us)
Async XLA Ops:
  7.2 1.6 copy-start
  10.1 107.6 %all-to-all-start = ((bf16[8,8,512]{2,1,0:T(8,128)(2,1)}), bf16[8,8,512]{2,1,0:T(8,128)(2,1)S(1)}, u32[]{:S(2)}, u32[]{:S(2)}) async-start(bf16[8,8,512]{2,1,0:T(8,128)(2,1)} %bitcast_select_fusion), calls=%async_computation | async-start | bytes 131072 | tf_op jit(solution)/shard_map/all_to_all | solution.py:47
  44.1 1.0 copy-start.3
  45.1 1.9 copy-start.1
  47.1 70.5 %copy-start.2 = (s32[768]{0:T(1024)S(1)}, s32[768]{0:T(1024)}, u32[]{:S(2)}) copy-start(s32[768]{0:T(1024)} %param.15) | copy-start | bytes 9220
  47.1 70.6 %copy-start.5 = (s32[2]{0:T(128)S(1)}, s32[2]{0:T(128)}, u32[]{:S(2)}) copy-start(s32[2]{0:T(128)} %param.17) | copy-start | bytes 28
  123.0 2.0 copy-start.4
  128.8 135.3 %all-to-all-start.1 = ((bf16[8,8,512]{2,1,0:T(8,128)(2,1)}), bf16[8,8,512]{2,1,0:T(8,128)(2,1)S(1)}, u32[]{:S(2)}, u32[]{:S(2)}) async-start(bf16[8,8,512]{2,1,0:T(8,128)(2,1)} %fusion.5), calls=%async_computation.1 | async-start | bytes 131072 | tf_op jit(solution)/shard_map/all_to_all | solution.py:80
  132.1 131.2 %all-reduce.3.cloned.1.call-start = ((), (), s32[]{:S(2)}) async-start(), calls=%async_computation.2 | async-start | bytes 262144
Sparse Core Ops, SparseCore 0:
  138.5 124.8 all-reduce.2
where the time goes:
time: 274 us
  waiting for transfers between devices  129 us (47%)
  blocking collectives  68.1 us (25%)
  other arithmetic  27.9 us (10%)
  matrix products  16.9 us (6%)
  between operations  14.2 us (5%)
  starting transfers between devices  10.7 us (4%)
  local copies, waits for them, and re-layouts  6.51 us (2%)
    unnamed x2, waiting for transfers between devices  129 us
    all_gather x1, blocking collectives, local(): lax.all_gather(hub_own, ('grp', 'dev'), axis=0, tiled=True)  68.1 us
    reduce_sum x6, other arithmetic, count_tiles(): return jnp.sum(matches.astype(jnp.bfloat16), axis=1)  22.4 us
    all_to_all x1, starting transfers between devices, local(): lax.all_to_all(outgoing, 'dev', split_axis=0, concat_axis=0, tiled=True)  7.31 us
  transfers between devices with their start and end apart: 3, of which 1 were waited for; matrix products, arithmetic and copies ran while one was open for 12% of the time, Pallas kernels for 0%

commit v1 on v0

--- a/solution.py
+++ b/solution.py
@@ -51,7 +51,9 @@
     tile_cols = tile_hub
     summed = summed + jnp.dot(
         tile_cols,
-        lax.all_gather(hub_own, ("grp", "dev"), axis=0, tiled=True),
+        lax.all_to_all(
+            jnp.tile(hub_own, (groups * members, 1)), ("grp", "dev"), split_axis=0, concat_axis=0, tiled=True
+        ),
         preferred_element_type=jnp.float32,
     )
     degree_f = degree.astype(jnp.float32)[:, None]
@@ -82,12 +84,9 @@
     ).astype(halo_partial.dtype)
     grad_total = grad_total + jax.ops.segment_sum(returned, send_list, num_segments=row_count)
     tile_cols = tile_hub
-    mine = lax.psum_scatter(
-        lax.dot_general(tile_cols, scaled, contract_first, preferred_element_type=jnp.float32),
-        ("grp", "dev"),
-        scatter_dimension=0,
-        tiled=True,
-    )
+    hub_partial = lax.dot_general(tile_cols, scaled, contract_first, preferred_element_type=jnp.float32)
+    arrived = lax.all_to_all(hub_partial, ("grp", "dev"), split_axis=0, concat_axis=0, tiled=True)
+    mine = jnp.sum(arrived.reshape(groups * members, owned_hubs, feat_width), axis=0)
     grad_total = grad_total + jax.ops.segment_sum(mine, hub_rows, num_segments=row_count)
     return (output, grad_total.astype(jnp.bfloat16))
 

time: 274 us -> 89.4 us (0.33)
  waiting for transfers between devices: 129 us -> 18.2 us
  blocking collectives: 68.1 us -> 0 us
  between operations: 14.2 us -> 0.82 us
  starting transfers between devices: 10.7 us -> 19.2 us
    unnamed x2 -> x0, waiting for transfers between devices: 129 us -> none
    all_gather x1 -> x0, blocking collectives: 68.1 us -> none  [local(): lax.all_gather(hub_own, ('grp', 'dev'), axis=0, tiled=True)]
    all_to_all x0 -> x2, waiting for transfers between devices: none -> 12.4 us  [the longest x1 6.89 us: local(): lax.all_to_all(jnp.tile(hub_own, (groups * members, 1)), ('grp', 'dev'),...]
    all_to_all x0 -> x2, starting transfers between devices: none -> 8.56 us  [the longest x1 6 us: local(): lax.all_to_all(jnp.tile(hub_own, (groups * members, 1)), ('grp', 'dev'),...]
    all_to_all x1, waiting for transfers between devices: 0.01 us -> 5.83 us  [local(): lax.all_to_all(halo_partial.astype(jnp.bfloat16), 'dev', split_axis=0, co...]
  transfers between devices with their start and end apart: 3 -> 4, of which waited for: 1 -> 3; matrix products, arithmetic and copies ran while one was open for 12% -> 39% of each run, Pallas kernels for 0% -> 0%
where the time goes in v1:
time: 89.4 us; the launch traced here: 88.9 us
  other arithmetic  27.9 us (31%)
  starting transfers between devices  19.2 us (21%)
  waiting for transfers between devices  18.2 us (20%)
  matrix products  16.2 us (18%)
  local copies, waits for them, and re-layouts  6.24 us (7%)
    reduce_sum x6, other arithmetic, count_tiles(): return jnp.sum(matches.astype(jnp.bfloat16), axis=1)  22.3 us
    all_to_all x1, starting transfers between devices, local(): lax.all_to_all(outgoing, 'dev', split_axis=0, concat_axis=0, tiled=True)  7.31 us
    all_to_all x1, waiting for transfers between devices, local(): lax.all_to_all(jnp.tile(hub_own, (groups * members, 1)), ('grp', 'dev'),...  6.89 us
    all_to_all x1, starting transfers between devices, local(): lax.all_to_all(jnp.tile(hub_own, (groups * members, 1)), ('grp', 'dev'),...  6 us
    all_to_all x1, waiting for transfers between devices, local(): lax.all_to_all(halo_partial.astype(jnp.bfloat16), 'dev', split_axis=0, co...  5.83 us
    all_to_all x1, waiting for transfers between devices, local(): lax.all_to_all(hub_partial, ('grp', 'dev'), split_axis=0, concat_axis=0,...  5.52 us
    dot_general x1, matrix products, local(): jnp.dot(neigh_mean, w_neigh, preferred_element_type=jnp.float32)  4.81 us
    all_to_all x1, starting transfers between devices, local(): lax.all_to_all(halo_partial.astype(jnp.bfloat16), 'dev', split_axis=0, co...  3.35 us
  transfers between devices with their start and end apart: 4, of which 3 were waited for; matrix products, arithmetic and copies ran while one was open for 39% of the time, Pallas kernels for 0%

profile of v1, /device:TPU:0, one launch (start us, length us, event | category | flops | bytes accessed | tf_op | source)
XLA Modules:
  0.0 88.9 jit_solution(4157572997564963641)
XLA Ops:
  0.6 0.8 reshape.119
  1.5 0.7 compare_and_fusion
  2.2 0.7 gather_fusion
  2.9 0.7 bitcast_select_fusion
  3.6 7.3 %all-to-all-start = ((bf16[8,8,512]{2,1,0:T(8,128)(2,1)}), bf16[8,8,512]{2,1,0:T(8,128)(2,1)S(1)}, u32[]{:S(2)}, u32[]{:S(2)}) async-start(bf16[8,8,512]{2,1,0:T(8,128)(2,1)} %bitcast_select_fusion), calls=%async_computation | async-start | bytes 131072 | tf_op jit(solution)/shard_map/all_to_all | solution.py:47
  11.6 0.7 compare_and_fusion.1
  12.3 0.9 %reshape.116 = s32[3,256,32]{1,0,2:T(4,128)S(1)} reshape(s32[768,32]{0,1:T(8,128)} %param.14) | data formatting | bytes 196608 | tf_op jit(solution)/shard_map/reshape | solution.py:38
  13.2 0.7 lt.49
  13.9 23.6 %while.17 = (s32[]{:T(128)}, bf16[3,256,768]{2,1,0:T(8,128)(2,1)S(1)}, bf16[3,256,64]{1,2,0:T(8,128)(2,1)S(1)}, bf16[3,256,64]{1,2,0:T(8,128)(2,1)S(1)}, s32[3,2...) while((s32[]{:T(128)}, bf16[3,256,768]{2,1,0:T(8,128)(2,1)S(1)}, ...), condition=%wide.region_4.5_spmd, body=%wide.region_0.4_spmd.sunk | while | flops 29130880 | bytes 1688669 | solution.py:35
  14.0 0.8 fusion.39
  15.1 6.7 %fusion.38 = bf16[256,768]{1,0:T(8,128)(2,1)S(1)} fusion(s32[256,32]{1,0:T(8,128)S(1)} %bitcast.65, pred[256,32]{1,0:T(8,128)(4,1)S(1)} %copy.41), kind=kLoop, calls=%fused_computation.6.clone.1 | loop fusion | flops 24969216 | bytes 434176 | tf_op jit(solution)/shard_map/while/body/eval_jaxpr/reduce_sum | solution.py:12
  21.9 0.8 fusion.39
  22.9 6.7 %fusion.38 = bf16[256,768]{1,0:T(8,128)(2,1)S(1)} fusion(s32[256,32]{1,0:T(8,128)S(1)} %bitcast.65, pred[256,32]{1,0:T(8,128)(4,1)S(1)} %copy.41), kind=kLoop, calls=%fused_computation.6.clone.1 | loop fusion | flops 24969216 | bytes 434176 | tf_op jit(solution)/shard_map/while/body/eval_jaxpr/reduce_sum | solution.py:12
  29.7 0.8 fusion.39
  30.8 6.7 %fusion.38 = bf16[256,768]{1,0:T(8,128)(2,1)S(1)} fusion(s32[256,32]{1,0:T(8,128)S(1)} %bitcast.65, pred[256,32]{1,0:T(8,128)(4,1)S(1)} %copy.41), kind=kLoop, calls=%fused_computation.6.clone.1 | loop fusion | flops 24969216 | bytes 434176 | tf_op jit(solution)/shard_map/while/body/eval_jaxpr/reduce_sum | solution.py:12
  37.5 1.9 %fusion.18 = f32[768,512]{1,0:T(8,128)} fusion(bf16[768,768]{1,0:T(8,128)(2,1)S(1)} %bitcast.73, bf16[768,512]{1,0:T(8,128)(2,1)S(1)} %copy-done), kind=kOutput, calls=%fused_computation.52 | convolution fusion | flops 603979776 | bytes 3538944 | tf_op jit(solution)/shard_map/dot_general | solution.py:48
  39.5 1.7 %fusion.17 = f32[768,512]{1,0:T(8,128)} fusion(bf16[768,512]{1,0:T(8,128)(2,1)S(1)} %copy-done, bf16[512,512]{1,0:T(8,128)(2,1)S(1)} %copy-done.1), kind=kOutput, calls=%fused_computation.51 | convolution fusion | flops 402653184 | bytes 2883584 | tf_op jit(solution)/shard_map/dot_general | solution.py:61
  42.0 0.7 tile.2
  42.7 6.0 %all-to-all-start.1 = ((bf16[32,2,512]{2,1,0:T(2,128)(2,1)}), bf16[32,2,512]{2,1,0:T(2,128)(2,1)S(1)}, u32[]{:S(2)}, u32[]{:S(2)}) async-start(bf16[32,2,512]{2,1,0:T(2,128)(2,1)} %tile.2), calls=%async_computation.1 | async-start | bytes 131072 | tf_op jit(solution)/shard_map/all_to_all | solution.py:54
  49.1 6.9 %all-to-all-done.1 = bf16[32,2,512]{2,1,0:T(2,128)(2,1)S(1)} async-done(((bf16[32,2,512]{2,1,0:T(2,128)(2,1)}), bf16[32,2,512]{2,1,0:T(2,128)(2,1)S(1)}, u32[]{:S(2)}, u32[]{:S(2)}) %all-to-all-start.1) | async-done | bytes 65568 | tf_op jit(solution)/shard_map/all_to_all | solution.py:54
  56.0 4.8 %multiply_convert_fusion = (bf16[768,512]{1,0:T(8,128)(2,1)}, bf16[768,512]{1,0:T(8,128)(2,1)}) fusion(bf16[768,512]{1,0:T(8,128)(2,1)} %param.11, f32[768,512]{1,0:T(8,128)} %fusion.17, bf16[512,512]{1,0:T(8,128)(2,1)} %param.13, f32[768,512]{1,0:T(8,128)} %fusion.18, f32[768,512]{1,0:T(8,128)S(1)} %fusion.14, bf16[768,64]{0,1:T(8,128)(2,1)S(1)} %bitcast.70, ...), kind=kOutput, calls=%fused_computation.20 | convolution fusion | flops 459669504 | bytes 7769088 | tf_op jit(solution)/shard_map/dot_general | solution.py:61
  60.8 2.0 %divide_convert_fusion = bf16[768,512]{1,0:T(8,128)(2,1)S(1)} fusion(bf16[768,512]{1,0:T(8,128)(2,1)} %get-tuple-element.125, bf16[512,512]{1,0:T(8,128)(2,1)} %param.13, f32[768]{0:T(1024)S(1)} %convert_element_type.57), kind=kOutput, calls=%fused_computation.19 | convolution fusion | flops 403439616 | bytes 2100224 | tf_op jit(solution)/shard_map/dot_general | solution.py:73
  62.8 2.0 %fusion.19 = f32[768,512]{1,0:T(8,128)} fusion(bf16[768,768]{1,0:T(8,128)(2,1)S(1)} %bitcast.74, bf16[768,512]{1,0:T(8,128)(2,1)S(1)} %divide_convert_fusion), kind=kOutput, calls=%fused_computation.53 | convolution fusion | flops 603979776 | bytes 3538944 | tf_op jit(solution)/shard_map/dot_general | solution.py:76
  64.8 0.9 fusion.5
  65.7 3.3 %all-to-all-start.2 = ((bf16[8,8,512]{2,1,0:T(8,128)(2,1)}), bf16[8,8,512]{2,1,0:T(8,128)(2,1)S(1)}, u32[]{:S(2)}, u32[]{:S(2)}) async-start(bf16[8,8,512]{2,1,0:T(8,128)(2,1)} %fusion.5), calls=%async_computation.2 | async-start | bytes 131072 | tf_op jit(solution)/shard_map/all_to_all | solution.py:82
  69.3 0.8 copy.28
  70.0 5.8 %all-to-all-done.2 = bf16[8,8,512]{2,1,0:T(8,128)(2,1)S(1)} async-done(((bf16[8,8,512]{2,1,0:T(8,128)(2,1)}), bf16[8,8,512]{2,1,0:T(8,128)(2,1)S(1)}, u32[]{:S(2)}, u32[]{:S(2)}) %all-to-all-start.2) | async-done | bytes 65568 | tf_op jit(solution)/shard_map/all_to_all | solution.py:82
  75.9 2.6 %all-to-all-start.3 = ((f32[32,2,512]{2,1,0:T(2,128)}), f32[32,2,512]{2,1,0:T(2,128)S(1)}, u32[]{:S(2)}, u32[]{:S(2)}) async-start(f32[32,2,512]{2,1,0:T(2,128)} %copy.28), calls=%async_computation.3 | async-start | bytes 262144 | tf_op jit(solution)/shard_map/all_to_all | solution.py:88
  78.4 2.3 %convolution_add_fusion = f32[768,512]{1,0:T(8,128)S(1)} fusion(f32[768,512]{1,0:T(8,128)} %fusion.19, bf16[768,512]{1,0:T(8,128)(2,1)} %get-tuple-element.125, bf16[512,512]{1,0:T(8,128)(2,1)S(1)} %copy-done.1), kind=kOutput, calls=%fused_computation.24 | convolution fusion | flops 403046400 | bytes 4456448 | tf_op jit(solution)/shard_map/dot_general | solution.py:71
  80.7 5.5 %all-to-all-done.3 = f32[32,2,512]{2,1,0:T(2,128)S(1)} async-done(((f32[32,2,512]{2,1,0:T(2,128)}), f32[32,2,512]{2,1,0:T(2,128)S(1)}, u32[]{:S(2)}, u32[]{:S(2)}) %all-to-all-start.3) | async-done | bytes 131104 | tf_op jit(solution)/shard_map/all_to_all | solution.py:88
  86.3 1.6 %scatter_custom_fusion = f32[768,512]{1,0:T(8,128)S(1)} fusion(f32[768,512]{1,0:T(8,128)S(1)} %convolution_add_fusion, s32[66]{0:T(128)S(1)} %add_bitcast_fusion, f32[2,512]{1,0:T(2,128)S(1)} %reduce_sum.45, f32[]{:T(128)} %constant.86, f32[64,512]{1,0:T(8,128)S(1)} %bitcast_convert_fusion), kind=kCustom, calls=%fused_computation.31 | custom fusion | flops 67584 | bytes 1708036 | tf_op jit(solution)/shard_map/add | solution.py:90
  87.9 1.0 %convert_element_type.66 = bf16[768,512]{1,0:T(8,128)(2,1)} convert(f32[768,512]{1,0:T(8,128)S(1)} %scatter_custom_fusion) | non-fusion elementwise | flops 393216 | bytes 2359296 | tf_op jit(solution)/shard_map/convert_element_type | solution.py:91
  (60 shorter events, 3.2 us)
Async XLA Ops:
  0.6 1.6 %copy-start = (bf16[768,512]{1,0:T(8,128)(2,1)S(1)}, bf16[768,512]{1,0:T(8,128)(2,1)}, u32[]{:S(2)}) copy-start(bf16[768,512]{1,0:T(8,128)(2,1)} %param.10) | copy-start | bytes 2359300
  3.6 38.4 %all-to-all-start = ((bf16[8,8,512]{2,1,0:T(8,128)(2,1)}), bf16[8,8,512]{2,1,0:T(8,128)(2,1)S(1)}, u32[]{:S(2)}, u32[]{:S(2)}) async-start(bf16[8,8,512]{2,1,0:T(8,128)(2,1)} %bitcast_select_fusion), calls=%async_computation | async-start | bytes 131072 | tf_op jit(solution)/shard_map/all_to_all | solution.py:47
  37.5 2.0 %copy-start.3 = (bf16[3,256,768]{2,1,0:T(8,128)(2,1)}, bf16[3,256,768]{2,1,0:T(8,128)(2,1)S(1)}, u32[]{:S(2)}) copy-start(bf16[3,256,768]{2,1,0:T(8,128)(2,1)S(1)} %get-tuple-element.100) | copy-start | bytes 3538948
  37.5 1.9 %copy-start.1 = (bf16[512,512]{1,0:T(8,128)(2,1)S(1)}, bf16[512,512]{1,0:T(8,128)(2,1)}, u32[]{:S(2)}) copy-start(bf16[512,512]{1,0:T(8,128)(2,1)} %param.12) | copy-start | bytes 1572868
  39.5 2.4 %copy-start.2 = (s32[768]{0:T(1024)S(1)}, s32[768]{0:T(1024)}, u32[]{:S(2)}) copy-start(s32[768]{0:T(1024)} %param.15) | copy-start | bytes 9220
  39.5 2.5 %copy-start.5 = (s32[2]{0:T(128)S(1)}, s32[2]{0:T(128)}, u32[]{:S(2)}) copy-start(s32[2]{0:T(128)} %param.17) | copy-start | bytes 28
  42.7 13.3 %all-to-all-start.1 = ((bf16[32,2,512]{2,1,0:T(2,128)(2,1)}), bf16[32,2,512]{2,1,0:T(2,128)(2,1)S(1)}, u32[]{:S(2)}, u32[]{:S(2)}) async-start(bf16[32,2,512]{2,1,0:T(2,128)(2,1)} %tile.2), calls=%async_computation.1 | async-start | bytes 131072 | tf_op jit(solution)/shard_map/all_to_all | solution.py:54
  60.8 2.0 %copy-start.4 = (bf16[3,256,768]{2,1,0:T(8,128)(2,1)S(1)}, bf16[3,256,768]{2,1,0:T(8,128)(2,1)}, u32[]{:S(2)}) copy-start(bf16[3,256,768]{2,1,0:T(8,128)(2,1)} %copy-done.3) | copy-start | bytes 3538948
  65.7 10.2 %all-to-all-start.2 = ((bf16[8,8,512]{2,1,0:T(8,128)(2,1)}), bf16[8,8,512]{2,1,0:T(8,128)(2,1)S(1)}, u32[]{:S(2)}, u32[]{:S(2)}) async-start(bf16[8,8,512]{2,1,0:T(8,128)(2,1)} %fusion.5), calls=%async_computation.2 | async-start | bytes 131072 | tf_op jit(solution)/shard_map/all_to_all | solution.py:82
  75.9 10.4 %all-to-all-start.3 = ((f32[32,2,512]{2,1,0:T(2,128)}), f32[32,2,512]{2,1,0:T(2,128)S(1)}, u32[]{:S(2)}, u32[]{:S(2)}) async-start(f32[32,2,512]{2,1,0:T(2,128)} %copy.28), calls=%async_computation.3 | async-start | bytes 262144 | tf_op jit(solution)/shard_map/all_to_all | solution.py:88

commit v2 on v1

v2 whole, which is shorter than its diff:
```python
import functools

import jax
import jax.numpy as jnp
from jax import lax
from jax.experimental import pallas as pl
from jax.experimental.pallas import tpu as pltpu
from jax.sharding import PartitionSpec as P

MESH = pl.DeviceIdType.MESH
BF = jnp.bfloat16
F32 = jnp.float32
CODE = jnp.int16
PACK = 16


def dot(a, b, lhs_dim, rhs_dim):
    return lax.dot_general(a, b, (((lhs_dim,), (rhs_dim,)), ((), ())), preferred_element_type=F32)


def layer_kernel(
    groups, members, owned, tile_rows,
    x_ref, g_ref, ws_ref, wn_ref, codes_ref, deg_ref, send_ref, hub_ref,
    out_ref, grad_ref,
    counts, source, scaled, total, spread,
    halo_out, halo_in, back_out, back_in, hub_out, hub_in, sum_out, sum_in,
    send_sems, recv_sems,
):
    rows, feat = x_ref.shape
    slots = codes_ref.shape[0]
    devices = groups * members
    peer_rows = halo_out.shape[1]
    halo = members * peer_rows
    hubs = owned * devices
    first_hub = rows + halo
    columns = first_hub + hubs
    me_g, me_m = lax.axis_index("grp"), lax.axis_index("dev")
    me = me_g * members + me_m

    barrier = pltpu.get_barrier_semaphore()

    def greet(step, carry):
        t = lax.rem(me + step, devices)
        pl.semaphore_signal(barrier, inc=1, device_id=(t // members, lax.rem(t, members)), device_id_type=MESH)
        return carry

    lax.fori_loop(1, devices, greet, 0)

    row_ids = lax.broadcasted_iota(jnp.int32, (halo, rows), 1)
    pick_halo = jnp.where(row_ids == send_ref[...], 1.0, 0.0).astype(BF)
    halo_out[...] = dot(pick_halo, x_ref[...], 1, 0).reshape(members, peer_rows, feat)
    lane_ids = lax.broadcasted_iota(jnp.int32, (8, rows), 1)
    sub_ids = lax.broadcasted_iota(jnp.int32, (8, rows), 0)
    hub_mask = jnp.zeros((8, rows), F32)
    for j in range(owned):
        hub_mask = jnp.where((sub_ids == j) & (lane_ids == hub_ref[j]), 1.0, hub_mask)
    own = dot(hub_mask.astype(BF), x_ref[...], 1, 0)
    for j in range(owned):
        hub_out[0, :, j * feat:(j + 1) * feat] = own[j:j + 1, :]
    hub_in[me] = hub_out[0]
    halo_in[me_m] = halo_out[me_m]
    source[:rows, :] = x_ref[...]
    for k in range(slots):
        spread[k] = jnp.broadcast_to(codes_ref[k:k + 1, :], (PACK, rows)).astype(CODE)

    pl.semaphore_wait(barrier, devices - 1)

    def to_member(src, dst, sem):
        def body(step, carry):
            p = lax.rem(me_m + step, members)
            pltpu.make_async_remote_copy(
                src_ref=src.at[p], dst_ref=dst.at[me_m], send_sem=send_sems.at[sem], recv_sem=recv_sems.at[sem],
                device_id=(me_g, p), device_id_type=MESH,
            ).start()
            return carry
        lax.fori_loop(1, members, body, 0)

    def to_all(src, dst, sem, shared):
        def body(step, carry):
            t = lax.rem(me + step, devices)
            pltpu.make_async_remote_copy(
                src_ref=src.at[0 if shared else t], dst_ref=dst.at[me],
                send_sem=send_sems.at[sem], recv_sem=recv_sems.at[sem],
                device_id=(t // members, lax.rem(t, members)), device_id_type=MESH,
            ).start()
            return carry
        lax.fori_loop(1, devices, body, 0)

    def drain(buf, count, sem):
        view = buf.at[pl.ds(0, count)]
        pltpu.make_async_copy(view, view, recv_sems.at[sem]).wait()
        pltpu.make_async_copy(view, view, send_sems.at[sem]).wait()

    to_all(hub_out, hub_in, 1, True)
    to_member(halo_out, halo_in, 0)

    parts = tile_rows // PACK
    sub = lax.broadcasted_iota(jnp.int32, (PACK, rows), 0)

    def count_block(i, carry):
        base = pl.multiple_of(i * tile_rows, tile_rows)
        names = [(sub + (base + PACK * q)).astype(CODE) for q in range(parts)]
        one, zero = jnp.ones((PACK, rows), BF), jnp.zeros((PACK, rows), BF)
        sums = [zero] * parts
        for k in range(slots):
            code = spread[k]
            sums = [s + jnp.where(code == n, one, zero) for s, n in zip(sums, names)]
        for q in range(parts):
            counts[pl.ds(pl.multiple_of(base + PACK * q, PACK), PACK), :] = sums[q]
        return carry

    lax.fori_loop(0, columns // tile_rows, count_block, 0)

    drain(halo_in, members - 1, 0)
    drain(hub_in, devices - 1, 1)
    source[rows:first_hub, :] = halo_in[...].reshape(halo, feat).astype(BF)
    hub_rows_in = hub_in[...].reshape(devices, owned * feat)
    for j in range(owned):
        source[first_hub + j * devices:first_hub + (j + 1) * devices, :] = (
            hub_rows_in[:, j * feat:(j + 1) * feat].astype(BF))

    block = 256 if rows % 256 == 0 else rows
    blocks = rows // block

    def node_block(i, carry):
        at = pl.ds(pl.multiple_of(i * block, block), block)
        degree = deg_ref[at, :]
        mean = (dot(counts[:, at], source[...], 0, 0) / degree).astype(BF)
        pre = dot(x_ref[at, :], ws_ref[...], 1, 0) + dot(mean, wn_ref[...], 1, 0)
        sig = jax.nn.sigmoid(pre)
        out_ref[at, :] = (pre * sig).astype(BF)
        gated = (g_ref[at, :].astype(F32) * sig * (1.0 + pre * (1.0 - sig))).astype(BF)
        scaled[at, :] = (dot(gated, wn_ref[...], 1, 1) / degree).astype(BF)
        total[at, :] = dot(gated, ws_ref[...], 1, 1)
        return carry

    lax.fori_loop(0, blocks, node_block, 0)

    away = dot(counts[rows:, :], scaled[...], 1, 0)
    back_out[...] = away[:halo].reshape(members, peer_rows, feat)
    sum_out[...] = jnp.concatenate(
        [away[halo + j * devices:halo + (j + 1) * devices] for j in range(owned)], axis=1
    ).reshape(devices, 1, owned * feat)
    back_in[me_m] = back_out[me_m]
    sum_in[me] = sum_out[me]

    def local_block(i, carry):
        at = pl.ds(pl.multiple_of(i * block, block), block)
        total[at, :] += dot(counts[at, :], scaled[...], 1, 0)
        return carry

    lax.fori_loop(0, 1, local_block, 0)
    to_all(sum_out, sum_in, 3, False)
    to_member(back_out, back_in, 2)
    lax.fori_loop(1, blocks, local_block, 0)
    drain(back_in, members - 1, 2)
    drain(sum_in, devices - 1, 3)

    returned = back_in[...].reshape(halo, feat).astype(BF)
    mine = jnp.sum(sum_in[...], axis=0)

    def final_block(i, carry):
        at = pl.ds(pl.multiple_of(i * block, block), block)
        ids = lax.broadcasted_iota(jnp.int32, (halo, block), 1) + i * block
        place = jnp.where(ids == send_ref[...], 1.0, 0.0).astype(BF)
        value = total[at, :] + dot(place, returned, 0, 0)
        node_ids = lax.broadcasted_iota(jnp.int32, (block, feat), 0) + i * block
        for j in range(owned):
            value = value + jnp.where(node_ids == hub_ref[j], mine[:, j * feat:(j + 1) * feat], 0.0)
        grad_ref[at, :] = value.astype(BF)
        return carry

    lax.fori_loop(0, blocks, final_block, 0)


def local(groups, members, features, grad_out, w_self, w_neigh, neighbours, degree, send_rows, hub_rows):
    rows, feat = features.shape
    slots = neighbours.shape[1]
    devices = groups * members
    peer_rows = send_rows.shape[1]
    halo = send_rows.shape[0] * peer_rows
    owned = hub_rows.shape[0]
    hubs = owned * devices
    first_hub = rows + halo
    columns = first_hub + hubs
    h = neighbours - first_hub
    codes = jnp.where(h >= 0, first_hub + (h % owned) * devices + h // owned, neighbours)
    codes = jnp.where(lax.iota(jnp.int32, slots)[None, :] < degree[:, None], codes, -1).T
    vmem = pl.BlockSpec(memory_space=pltpu.VMEM)
    chunk = (members, peer_rows, feat)
    strip = (devices, 1, owned * feat)
    return pl.pallas_call(
        functools.partial(layer_kernel, groups, members, owned, 64),
        out_shape=(jax.ShapeDtypeStruct((rows, feat), BF), jax.ShapeDtypeStruct((rows, feat), BF)),
        in_specs=[vmem] * 7 + [pl.BlockSpec(memory_space=pltpu.SMEM)],
        out_specs=(vmem, vmem),
        scratch_shapes=[
            pltpu.VMEM((columns, rows), BF),
            pltpu.VMEM((columns, feat), BF),
            pltpu.VMEM((rows, feat), BF),
            pltpu.VMEM((rows, feat), F32),
            pltpu.VMEM((slots, PACK, rows), CODE),
            pltpu.VMEM(chunk, F32), pltpu.VMEM(chunk, F32), pltpu.VMEM(chunk, F32), pltpu.VMEM(chunk, F32),
            pltpu.VMEM((1, 1, owned * feat), F32), pltpu.VMEM(strip, F32), pltpu.VMEM(strip, F32), pltpu.VMEM(strip, F32),
            pltpu.SemaphoreType.DMA((4,)),
            pltpu.SemaphoreType.DMA((4,)),
        ],
        compiler_params=pltpu.CompilerParams(collective_id=0, has_side_effects=True),
    )(
        features, grad_out, w_self, w_neigh, codes,
        degree.astype(F32)[:, None], send_rows.reshape(halo, 1), hub_rows,
    )


def solution(mesh):
    both = ("grp", "dev")
    placed = (P(both, None), P(both, None), P(), P(), P(both, None), P(both), P(both, None), P(both))
    return jax.shard_map(
        functools.partial(local, mesh.shape["grp"], mesh.shape["dev"]),
        mesh=mesh,
        in_specs=placed,
        out_specs=(P(both, None), P(both, None)),
        check_vma=False,
    )
```

time: 89.4 us -> 37.8 us (0.42)
  Pallas kernels: 0 us -> 29.9 us
  other arithmetic: 27.9 us -> 2.34 us
  starting transfers between devices: 19.2 us -> 0 us
  waiting for transfers between devices: 18.2 us -> 0 us
  matrix products: 16.2 us -> 0 us
  local copies, waits for them, and re-layouts: 6.24 us -> 4.62 us
    pallas_call x0 -> x1, Pallas kernels: none -> 29.9 us  [local(): pl.pallas_call(functools.partial(layer_kernel, groups, members, owned, 64...]
    reduce_sum x7 -> x0, other arithmetic: 22.4 us -> none  [the longest x6 22.3 us: count_tiles(): return jnp.sum(matches.astype(jnp.bfloat16), axis=1)]
    all_to_all x4 -> x0, starting transfers between devices: 19.2 us -> none  [the longest x1 7.31 us: local(): lax.all_to_all(outgoing, 'dev', split_axis=0, concat_axis=0, tiled=True)]
    all_to_all x4 -> x0, waiting for transfers between devices: 18.2 us -> none  [the longest x1 6.89 us: local(): lax.all_to_all(jnp.tile(hub_own, (groups * members, 1)), ('grp', 'dev'),...]
    dot_general x9 -> x0, matrix products: 16.2 us -> none  [the longest x1 4.81 us: local(): jnp.dot(neigh_mean, w_neigh, preferred_element_type=jnp.float32)]
    unnamed x12 -> x8, local copies, waits for them, and re-layouts: 0.03 us -> 3.03 us
    transpose x0 -> x1, other arithmetic: none -> 1.65 us  [local(): jnp.where(lax.iota(jnp.int32, slots)[None, :] < degree[:, None], codes, -1)]
    add x7 -> x0, other arithmetic: 1.6 us -> none  [the longest x1 1.58 us: local(): grad_total + jax.ops.segment_sum(mine, hub_rows, num_segments=row_count)]
  transfers between devices with their start and end apart: 4 -> 0, of which waited for: 3 -> 0; matrix products, arithmetic and copies ran while one was open for 39% -> 0% of each run, Pallas kernels for 0% -> 0%
where the time goes in v2:
time: 37.8 us; the launch traced here: 37.5 us
  Pallas kernels  29.9 us (79%)
  local copies, waits for them, and re-layouts  4.62 us (12%)
  other arithmetic  2.34 us (6%)
  between operations  0.66 us (2%)
    pallas_call x1, Pallas kernels, local(): pl.pallas_call(functools.partial(layer_kernel, groups, members, owned, 64...  29.9 us
    unnamed x8, local copies, waits for them, and re-layouts  3.03 us
    transpose x1, other arithmetic, local(): jnp.where(lax.iota(jnp.int32, slots)[None, :] < degree[:, None], codes, -1)  1.65 us
    broadcast_in_dim x1, local copies, waits for them, and re-layouts, local(): degree.astype(F32)[:, None]  0.91 us

profile of v2, /device:TPU:0, one launch (start us, length us, event | category | flops | bytes accessed | tf_op | source)
XLA Modules:
  0.0 37.5 jit_solution(15403841942742959870)
XLA Ops:
  0.6 0.0 copy-start.2
  0.6 0.7 %convert_element_type.3 = f32[768]{0:T(1024)S(1)} convert(s32[768]{0:T(1024)} %param.13) | non-fusion elementwise | flops 768 | bytes 6144 | tf_op jit(solution)/shard_map/convert_element_type | solution.py:211
  1.3 0.0 copy-done.2
  1.3 0.0 copy-start.1
  1.3 0.7 %reshape.9.send_ref = s32[64,1]{1,0:T(8,128)} reshape(s32[8,8]{1,0:T(8,128)S(1)} %copy-done.2) | data formatting | bytes 512 | tf_op jit(solution)/shard_map/reshape | solution.py:211
  2.0 0.0 copy-done.1
  2.0 1.6 %fusion.5.codes_ref = s32[32,768]{1,0:T(8,128)} fusion(s32[768,32]{0,1:T(8,128)} %param.12, s32[768]{0:T(1024)S(1)} %copy-done.1), kind=kLoop, calls=%fused_computation.10 | loop fusion | flops 663552 | bytes 199680 | tf_op jit(solution)/shard_map/transpose | solution.py:188
  3.7 0.9 %broadcast_in_dim.8.deg_ref = f32[768,1]{1,0:T(8,128)} reshape(f32[768]{0:T(1024)S(1)} %convert_element_type.3) | data formatting | bytes 6144 | tf_op jit(solution)/shard_map/broadcast_in_dim | solution.py:211
  4.6 29.9 %shard_map.95 = (bf16[768,512]{1,0:T(8,128)(2,1)}, bf16[768,512]{1,0:T(8,128)(2,1)}) custom-call(bf16[768,512]{1,0:T(8,128)(2,1)} %x_ref.1, bf16[768,512]{1,0:T(8,128)(2,1)} %g_ref.1, bf16[512,512]{1,0:T(8,128)(2,1)} %ws_ref.1, bf16[512,512]{1,0:T(8,128)(2,1)} %wn_ref.1, s32[32,768]{1,0:T(8,128)} %fusion.5.codes_ref, f32[768,1]{1,0:T(8,128)} %broadcast_in_dim.8.deg_ref, ...), custom_call_target="tpu_custom_call" | custom-call | tf_op jit(solution)/shard_map/pallas_call | solution.py:192
  34.5 0.0 copy-start
  34.5 2.1 %copy.15 = bf16[768,512]{1,0:T(8,128)(2,1)} copy(bf16[768,512]{1,0:T(8,128)(2,1)} %get-tuple-element.4) | data formatting | bytes 1572864
  36.6 0.0 copy-done
  36.6 0.9 %copy.16 = bf16[768,512]{1,0:T(8,128)(2,1)} copy(bf16[768,512]{1,0:T(8,128)(2,1)S(1)} %copy-done) | data formatting | bytes 1572864
Async XLA Ops:
  0.6 0.7 %copy-start.2 = (s32[8,8]{1,0:T(8,128)S(1)}, s32[8,8]{1,0:T(8,128)}, u32[]{:S(2)}) copy-start(s32[8,8]{1,0:T(8,128)} %param.14) | copy-start | bytes 772
  1.3 0.7 %copy-start.1 = (s32[768]{0:T(1024)S(1)}, s32[768]{0:T(1024)}, u32[]{:S(2)}) copy-start(s32[768]{0:T(1024)} %param.13) | copy-start | bytes 9220
  34.5 2.1 %copy-start = (bf16[768,512]{1,0:T(8,128)(2,1)S(1)}, bf16[768,512]{1,0:T(8,128)(2,1)}, u32[]{:S(2)}) copy-start(bf16[768,512]{1,0:T(8,128)(2,1)} %get-tuple-element.5) | copy-start | bytes 2359300
